TPU v7x, 32 devices: a whole 2x2x4 slice. The times are simulated.
32 devices in a mesh: ma: 16 (over z, y, x), ch: 2 (over core).
Axes of the slice: x: 2, y: 2, z: 4, core: 2. Of those that a mesh axis runs over, the one named last changes fastest.
Arguments:
- visibilities: bfloat16 [512, 512, 2, 128], P('ma', 'ch'), may hold values from -6 to 6
- kl_basis: bfloat16 [512, 256, 2, 512], P('ma', 'ch'), may hold values from -0.1875 to 0.1875
- time_flags: int32 [512], P('ma'), may hold values 0 or 1
Outputs:
- kl_modes: bfloat16 [512, 256, 2, 128], P('ma', 'ch')
All inputs are finite; a program needn't handle non-finite values. No bound on the sum of `time_flags` on one device may be relied on, other than what follows from the above.
Results may differ from a plain program's by a relative error of at most 0.006.
Values may be sent and summed in bfloat16 or wider, within the bound.
No kernel may reach another device: no remote copies, remote signals or barrier semaphores. Data moves between devices by JAX's collectives and lax.ppermute only.
A program may use at most 128 MiB of HBM per device.

v0:
```python
import math
import jax
import jax.numpy as jnp
from jax import lax
from jax.sharding import PartitionSpec as P

H = 128


def tap_table(offsets, total):
    shifts = jnp.mod(jnp.arange(2 * H + 1, dtype=jnp.int32) - H, total)
    phase_index = jnp.mod(shifts[:, None] * offsets[None, :], total)
    phases = phase_index.astype(jnp.float32) * (2.0 * math.pi / total)
    return (jnp.cos(phases), jnp.sin(phases))


def toeplitz(kernel_taps, block_rows):
    width = kernel_taps.shape[1]
    span = block_rows + width - 1
    reverse = kernel_taps[:, ::-1]
    padded = jnp.concatenate([reverse, jnp.zeros((2, block_rows), kernel_taps.dtype)], axis=1)
    tiled = jnp.tile(padded, (1, block_rows))[:, : block_rows * span].reshape(2, block_rows, span)
    real_part = tiled[0]
    imag_part = tiled[1]
    first = jnp.stack([real_part, -imag_part], 1)
    second = jnp.stack([imag_part, real_part], 1)
    return jnp.stack([first, second], 0)


def on_device(visibilities, kl_basis, time_flags):
    rows_dev = visibilities.shape[0]
    chan_dev = visibilities.shape[1]
    svd_modes = visibilities.shape[3]
    total = rows_dev * lax.axis_size("ma")
    all_flags = lax.all_gather(time_flags, "ma", axis=0, tiled=True)
    cosine, sine_table = tap_table(jnp.arange(total, dtype=jnp.int32), total)
    flag_values = all_flags.astype(jnp.float32)
    real_sum = jnp.dot(cosine, flag_values, precision=lax.Precision.HIGHEST)
    imag_sum = jnp.dot(sine_table, flag_values, precision=lax.Precision.HIGHEST)
    kernel_taps = (jnp.stack([real_sum, -imag_sum]) / total).astype(jnp.bfloat16)
    flat_rows = jnp.transpose(visibilities, (0, 2, 1, 3)).reshape(rows_dev, 2, chan_dev * svd_modes)
    columns = lax.all_to_all(flat_rows, "ma", split_axis=2, concat_axis=0, tiled=True)
    block_rows = math.gcd(total, 128)
    toeplitz_block = toeplitz(kernel_taps, block_rows)
    wrapped = jnp.concatenate([columns[total - H :], columns, columns[:H]], axis=0)

    def convolve(block_index):
        window = lax.dynamic_slice_in_dim(wrapped, block_index * block_rows, block_rows + 2 * H, 0)
        return jnp.einsum(
            "pbqe,eqf->bpf", toeplitz_block, window, preferred_element_type=jnp.float32
        ).astype(jnp.bfloat16)

    mixed_blocks = lax.map(convolve, jnp.arange(total // block_rows, dtype=jnp.int32))
    mixed_columns = mixed_blocks.reshape(total, 2, columns.shape[2])
    returned = lax.all_to_all(mixed_columns, "ma", split_axis=0, concat_axis=2, tiled=True)
    mixed_rows = jnp.transpose(returned.reshape(rows_dev, 2, chan_dev, svd_modes), (0, 2, 1, 3))
    products = jnp.einsum(
        "mkqc,mcrs->mkqrs",
        kl_basis,
        lax.all_gather(mixed_rows, "ch", axis=1, tiled=True),
        preferred_element_type=jnp.float32,
    )
    real_out = products[:, :, 0, 0, :] - products[:, :, 1, 1, :]
    imag_out = products[:, :, 0, 1, :] + products[:, :, 1, 0, :]
    return jnp.stack([real_out, imag_out], 2).astype(jnp.bfloat16)


def solution(mesh):
    return jax.shard_map(
        on_device,
        mesh=mesh,
        in_specs=(P("ma", "ch", None, None), P("ma", "ch", None, None), P("ma")),
        out_specs=P("ma", "ch", None, None),
        check_vma=False,
    )
```

profile of v0, /device:TPU:0, one launch (start us, length us, event | category | flops | bytes accessed | tf_op | source)
XLA Modules:
  0.0 460.7 jit_solution(17408753481748408428)
XLA Ops:
  6.5 40.5 %copy.49 = bf16[32,2,256,128]{0,1,3,2:T(2,128)(2,1)} copy(bf16[32,2,256,128]{3,1,2,0:T(2,128)(2,1)} %bitcast.99) | data formatting | bytes 8388608 | tf_op jit(solution)/shard_map/reshape | solution.py:41
  47.0 20.8 %reshape.107 = bf16[16,2,65536]{2,1,0:T(2,128)(2,1)} reshape(bf16[32768,2,32]{2,1,0:T(2,128)(2,1)} %bitcast.92) | data formatting | bytes 8388608
  67.8 0.0 copy-start.2
  67.8 0.0 copy-start.1
  67.8 8.5 %all-to-all-start = ((bf16[16,2,65536]{2,1,0:T(2,128)(2,1)}), bf16[16,2,65536]{2,1,0:T(2,128)(2,1)}, u32[]{:S(2)}, u32[]{:S(2)}) async-start(bf16[16,2,65536]{2,1,0:T(2,128)(2,1)} %reshape.107), calls=%async_computation | async-start | bytes 8388608 | tf_op jit(solution)/shard_map/all_to_all | solution.py:42
  76.3 0.0 all-gather.2.cloned.1.call-start
  76.4 0.0 copy-done.2
  76.4 0.6 dynamic-slice
  77.5 0.0 copy-done.1
  77.5 0.2 dynamic-update-slice
  77.8 91.8 %all-reduce.1 = s32[512]{0:T(512)S(1)} all-reduce(s32[512]{0:T(512)S(1)} %dynamic-update-slice), channel_id=1, replica_groups=mesh['ma'=16,'ch'=2] {'ma'}, use_global_device_ids=true, to_apply=%add.1 | all-reduce | flops 512 | bytes 4096
  169.6 2.6 convolution_reduce_fusion
  172.2 2.5 fusion.30
  174.8 0.5 reverse
  175.3 0.1 slice.75
  175.4 0.7 tile.10
  176.1 1.0 slice_reduce_fusion
  177.1 0.1 squeeze.4
  177.2 0.1 stack_squeeze.2
  177.4 0.0 all-to-all-done
  177.4 16.0 %reshape.108 = bf16[32768,2,32]{2,1,0:T(2,128)(2,1)} reshape(bf16[16,2,65536]{2,1,0:T(2,128)(2,1)} %all-to-all-done) | data formatting | bytes 8388608
  193.4 24.9 %copy.50 = bf16[32,2,16,2048]{3,2,0,1:T(8,128)(2,1)} copy(bf16[32,2,16,2048]{0,1,3,2:T(2,128)(2,1)} %bitcast.90) | data formatting | bytes 8388608 | tf_op jit(solution)/shard_map/all_to_all | solution.py:42
  218.3 38.2 %copy.51 = bf16[32,2,16,2048]{3,0,2,1:T(8,128)(2,1)} copy(bf16[32,2,16,2048]{0,1,3,2:T(2,128)(2,1)} %bitcast.91) | data formatting | bytes 8388608 | tf_op jit(solution)/shard_map/all_to_all | solution.py:42
  256.5 0.0 copy-start
  256.5 3.6 fusion.47
  260.1 0.6 copy.34
  260.7 0.6 copy.36
  261.2 0.0 copy-done
  261.3 7.0 %pad_maximum_fusion = bf16[768,2,2048]{2,0,1:T(8,128)(2,1)} fusion(bf16[128,2,2048]{2,0,1:T(8,128)(2,1)S(1)} %bitcast.101, bf16[512,2,2048]{2,0,1:T(8,128)(2,1)S(1)} %bitcast.93, bf16[128,2,2048]{2,0,1:T(8,128)(2,1)S(1)} %bitcast.100), kind=kLoop, calls=%fused_computation.11 | loop fusion | flops 18874368 | bytes 12582912 | tf_op jit(solution)/shard_map/concatenate | solution.py:45
  268.3 23.2 %while.10 = (s32[]{:T(128)}, bf16[4,128,2,2048]{3,1,0,2:T(8,128)(2,1)}, s32[4]{0:T(128)S(1)}, bf16[768,2,2048]{2,0,1:T(8,128)(2,1)}, bf16[2,128,2,384]{3,1,2,0:T...) while((s32[]{:T(128)}, bf16[4,128,2,2048]{3,1,0,2:T(8,128)(2,1)}, s32[4]{0:T(128)S(1)}, ...), condition=%wide.region_1.2_spmd, body=%wide.region_0.1_spmd.sunk | while | flops 805830656 | bytes 8782491 | solution.py:53
  268.3 0.6 dynamic_slice.20
  269.5 2.9 fusion.56
  272.5 0.5 copy.68
  273.0 1.1 constant_dynamic-update-slice_fusion.2
  274.1 0.6 dynamic_slice.20
  275.3 2.9 fusion.56
  278.3 0.5 copy.68
  278.8 1.1 constant_dynamic-update-slice_fusion.2
  279.9 0.6 dynamic_slice.20
  281.1 2.9 fusion.56
  284.1 0.5 copy.68
  284.6 1.1 constant_dynamic-update-slice_fusion.2
  285.7 0.6 dynamic_slice.20
  286.9 2.9 fusion.56
  289.9 0.5 copy.68
  290.4 1.1 constant_dynamic-update-slice_fusion.2
  291.5 6.5 %copy.39 = bf16[512,2,2048]{2,1,0:T(2,128)(2,1)S(1)} copy(bf16[512,2,2048]{2,0,1:T(8,128)(2,1)} %bitcast.102) | data formatting | bytes 8388608 | tf_op jit(solution)/shard_map/reshape | solution.py:54
  298.0 99.6 %all_to_all.33 = bf16[512,2,2048]{2,1,0:T(2,128)(2,1)S(1)} all-to-all(bf16[512,2,2048]{2,1,0:T(2,128)(2,1)S(1)} %copy.39), channel_id=1, replica_groups=mesh['ma'=16,'ch'=2] {'ma'}, dimensions={0} | all-to-all | bytes 8388608 | tf_op jit(solution)/shard_map/all_to_all | solution.py:55
  397.6 5.4 %copy.66 = bf16[16,32,2,2048]{3,0,2,1:T(8,128)(2,1)} copy(bf16[16,32,2,2048]{3,2,1,0:T(2,128)(2,1)S(1)} %bitcast.95) | data formatting | bytes 8388608 | tf_op jit(solution)/shard_map/all_to_all | solution.py:55
  403.0 7.4 %reshape.89 = bf16[32,2,256,128]{3,2,1,0:T(8,128)(2,1)} reshape(bf16[32,2,16,2048]{3,2,1,0:T(8,128)(2,1)} %bitcast.96) | data formatting | bytes 8388608 | tf_op jit(solution)/shard_map/reshape | solution.py:56
  410.4 6.5 %copy.41 = bf16[32,2,256,128]{2,3,1,0:T(8,128)(2,1)} copy(bf16[32,2,256,128]{3,2,1,0:T(8,128)(2,1)} %reshape.89) | data formatting | bytes 8388608 | tf_op jit(solution)/shard_map/reshape | solution.py:56
  416.9 0.0 all-gather.2.cloned.1.call-update
  416.9 16.5 %all-gather.2.cloned.1.call-done = bf16[32,512,2,128]{1,3,2,0:T(8,128)(2,1)} async-done(((bf16[32,256,2,128]{1,3,2,0:T(8,128)(2,1)}), bf16[32,512,2,128]{1,3,2,0:T(8,128)(2,1)}) %all-gather.2.cloned.1.call-update) | async-done | bytes 8388624 | tf_op jit(solution)/shard_map/all_gather | solution.py:60
  433.4 11.4 %fusion.16 = f32[32,128,2,2,128]{1,4,2,3,0:T(8,128)} fusion(bf16[32,128,2,512,1]{3,2,1,0,4:T(2,128)(2,1)} %bitcast.98, bf16[32,512,2,128]{1,3,2,0:T(8,128)(2,1)} %all-gather.2.cloned.1.call-done), kind=kOutput, calls=%fused_computation.13 | convolution fusion | flops 2147483648 | bytes 25165824 | tf_op jit(solution)/shard_map/mkqc,mcrs->mkqrs/dot_general | solution.py:57
  444.8 2.6 fusion.24
  447.3 2.6 fusion.25
  449.9 0.2 pad_maximum_fusion.1
  450.1 3.8 copy.45
  (13 shorter events, 0.2 us)
Async XLA Ops:
  67.8 8.6 %copy-start.2 = (u32[32]{0:T(128)S(1)}, u32[32]{0:T(128)}, u32[]{:S(2)}) copy-start(u32[32]{0:T(128)} %constant.52) | copy-start | bytes 388
  67.8 9.8 %copy-start.1 = (s32[32]{0:T(128)S(1)}, s32[32]{0:T(128)}, u32[]{:S(2)}) copy-start(s32[32]{0:T(128)} %param.7) | copy-start | bytes 388
  67.8 109.6 %all-to-all-start = ((bf16[16,2,65536]{2,1,0:T(2,128)(2,1)}), bf16[16,2,65536]{2,1,0:T(2,128)(2,1)}, u32[]{:S(2)}, u32[]{:S(2)}) async-start(bf16[16,2,65536]{2,1,0:T(2,128)(2,1)} %reshape.107), calls=%async_computation | async-start | bytes 8388608 | tf_op jit(solution)/shard_map/all_to_all | solution.py:42
  76.3 357.1 %all-gather.2.cloned.1.call-start = ((), (), s32[]{:S(2)}) async-start(), calls=%async_computation.2 | async-start | bytes 12582912 | tf_op jit(solution)/shard_map/all_gather | solution.py:60
  256.5 4.7 %copy-start = (bf16[32,2,16,2048]{3,0,2,1:T(8,128)(2,1)S(1)}, bf16[32,2,16,2048]{3,0,2,1:T(8,128)(2,1)}, u32[]{:S(2)}) copy-start(bf16[32,2,16,2048]{3,0,2,1:T(8,128)(2,1)} %copy.51) | copy-start | bytes 12582916
Sparse Core Ops, SparseCore 0:
  417.0 16.2 all-gather.1
where the time goes:
time: 467 us; the launch traced here: 461 us
  blocking collectives  191 us (41%)
  local copies, waits for them, and re-layouts  187 us (40%)
  matrix products  28.3 us (6%)
  waiting for transfers between devices  16.5 us (4%)
  between operations  14.2 us (3%)
  other arithmetic  12.5 us (3%)
  starting transfers between devices  8.56 us (2%)
    all_to_all x1, blocking collectives, on_device(): lax.all_to_all(mixed_columns, 'ma', split_axis=0, concat_axis=2, tiled=True)  99.6 us
    unnamed x1, blocking collectives  91.8 us
    all_to_all x2, local copies, waits for them, and re-layouts, on_device(): lax.all_to_all(flat_rows, 'ma', split_axis=2, concat_axis=0, tiled=True)  63.1 us
    reshape x1, local copies, waits for them, and re-layouts, on_device(): jnp.transpose(visibilities, (0, 2, 1, 3))  40.5 us
    unnamed x13, local copies, waits for them, and re-layouts  38.2 us
    all_gather x1, waiting for transfers between devices, on_device(): lax.all_gather(mixed_rows, 'ch', axis=1, tiled=True)  16.5 us
    reshape x2, local copies, waits for them, and re-layouts, on_device(): returned.reshape(rows_dev, 2, chan_dev, svd_modes)  13.9 us
    dot_general x4, matrix products, convolve(): jnp.einsum('pbqe,eqf->bpf', toeplitz_block, window, preferred_element_typ...  11.7 us
  transfers between devices with their start and end apart: 2, of which 1 were waited for; matrix products, arithmetic and copies ran while one was open for 2% of the time, Pallas kernels for 0%

commit v1 on v0

--- a/solution.py
+++ b/solution.py
@@ -3,6 +3,7 @@
 import jax.numpy as jnp
 from jax import lax
 from jax.sharding import PartitionSpec as P
+from jax.lax import all_to_all, axis_size
 
 H = 128
 
@@ -39,7 +40,10 @@
     imag_sum = jnp.dot(sine_table, flag_values, precision=lax.Precision.HIGHEST)
     kernel_taps = (jnp.stack([real_sum, -imag_sum]) / total).astype(jnp.bfloat16)
     flat_rows = jnp.transpose(visibilities, (0, 2, 1, 3)).reshape(rows_dev, 2, chan_dev * svd_modes)
-    columns = lax.all_to_all(flat_rows, "ma", split_axis=2, concat_axis=0, tiled=True)
+    columns = jnp.concatenate(
+        all_to_all(jnp.stack(jnp.split(flat_rows, axis_size("ma"), axis=2), axis=0), "ma", 0, 0),
+        axis=0,
+    )
     block_rows = math.gcd(total, 128)
     toeplitz_block = toeplitz(kernel_taps, block_rows)
     wrapped = jnp.concatenate([columns[total - H :], columns, columns[:H]], axis=0)

time: 467 us -> 361 us (0.77); the launches traced: 461 us -> 360 us
  local copies, waits for them, and re-layouts: 187 us -> 85.5 us
    all_to_all x2 -> x1, local copies, waits for them, and re-layouts: 63.1 us -> 2.5 us  [on_device(): all_to_all(jnp.stack(jnp.split(flat_rows, axis_size('ma'), axis=2), axis=...]
    reshape x1, local copies, waits for them, and re-layouts: 40.5 us -> 7.31 us  [on_device(): jnp.transpose(visibilities, (0, 2, 1, 3))]
    unnamed x13 -> x24, local copies, waits for them, and re-layouts: 38.2 us -> 26.4 us
    transpose x0 -> x1, local copies, waits for them, and re-layouts: none -> 5.23 us  [on_device(): jnp.transpose(visibilities, (0, 2, 1, 3))]
where the time goes in v1:
time: 361 us; the launch traced here: 360 us
  blocking collectives  191 us (53%)
  local copies, waits for them, and re-layouts  85.5 us (24%)
  matrix products  28.3 us (8%)
  waiting for transfers between devices  16.5 us (5%)
  between operations  14.2 us (4%)
  other arithmetic  12.6 us (3%)
  starting transfers between devices  8.56 us (2%)
    all_to_all x1, blocking collectives, on_device(): lax.all_to_all(mixed_columns, 'ma', split_axis=0, concat_axis=2, tiled=True)  99.6 us
    unnamed x1, blocking collectives  91.7 us
    unnamed x24, local copies, waits for them, and re-layouts  26.4 us
    all_gather x1, waiting for transfers between devices, on_device(): lax.all_gather(mixed_rows, 'ch', axis=1, tiled=True)  16.4 us
    reshape x2, local copies, waits for them, and re-layouts, on_device(): returned.reshape(rows_dev, 2, chan_dev, svd_modes)  13.8 us
    dot_general x4, matrix products, convolve(): jnp.einsum('pbqe,eqf->bpf', toeplitz_block, window, preferred_element_typ...  11.8 us
    dot_general x1, matrix products, on_device(): jnp.einsum('mkqc,mcrs->mkqrs', kl_basis, lax.all_gather(mixed_rows, 'ch',...  11.4 us
    all_to_all x1, starting transfers between devices, on_device(): all_to_all(jnp.stack(jnp.split(flat_rows, axis_size('ma'), axis=2), axis=...  8.52 us
  transfers between devices with their start and end apart: 2, of which 1 were waited for; matrix products, arithmetic and copies ran while one was open for 2% of the time, Pallas kernels for 0%

profile of v1, /device:TPU:0, one launch (start us, length us, event | category | flops | bytes accessed | tf_op | source)
XLA Modules:
  0.0 359.7 jit_solution(7885117892029958529)
XLA Ops:
  6.5 5.2 %copy.35 = bf16[32,2,256,128]{3,2,0,1:T(8,128)(2,1)} copy(bf16[32,2,256,128]{3,1,2,0:T(2,128)(2,1)} %bitcast.158) | data formatting | bytes 8388608 | tf_op jit(solution)/shard_map/transpose | solution.py:42
  11.8 7.3 %reshape.90 = bf16[32,2,32768]{2,0,1:T(8,128)(2,1)} reshape(bf16[32,2,256,128]{3,2,0,1:T(8,128)(2,1)} %copy.35) | data formatting | bytes 8388608 | tf_op jit(solution)/shard_map/reshape | solution.py:42
  19.1 1.7 fusion.52
  20.8 1.7 fusion.51
  22.4 1.7 fusion.50
  24.1 1.7 fusion.49
  25.8 1.7 fusion.48
  27.5 1.7 fusion.47
  29.1 1.7 fusion.46
  30.8 1.7 fusion.45
  32.5 1.7 fusion.44
  34.1 1.7 fusion.43
  35.8 1.7 fusion.42
  37.5 1.7 fusion.41
  39.2 1.7 fusion.40
  40.8 1.7 fusion.39
  42.5 1.7 fusion.38
  44.1 1.7 fusion.37
  45.8 8.5 %all-to-all-start = ((bf16[16,32,2,2048]{3,1,2,0:T(8,128)(2,1)}), bf16[16,32,2,2048]{3,1,2,0:T(8,128)(2,1)}, u32[]{:S(2)}, u32[]{:S(2)}) async-start(bf16[16,32,2,2048]{3,1,2,0:T(8,128)(2,1)} %fusion.37), calls=%async_computation | async-start | bytes 8388608 | tf_op jit(solution)/shard_map/all_to_all | solution.py:44
  54.4 0.0 all-gather.2.cloned.1.call-start
  54.4 0.6 dynamic-slice
  55.7 0.2 dynamic-update-slice
  55.9 91.7 %all-reduce.1 = s32[512]{0:T(512)S(1)} all-reduce(s32[512]{0:T(512)S(1)} %dynamic-update-slice), channel_id=1, replica_groups=mesh['ma'=16,'ch'=2] {'ma'}, use_global_device_ids=true, to_apply=%add.1 | all-reduce | flops 512 | bytes 4096
  147.6 2.6 convolution_reduce_fusion
  150.3 2.5 fusion.30
  152.8 0.5 reverse
  153.3 0.1 slice.75
  153.4 0.7 tile.10
  154.1 1.0 slice_reduce_fusion
  155.2 0.1 squeeze.4
  155.3 0.1 stack_squeeze.2
  155.4 1.7 fusion.63
  157.1 0.1 copy.36
  157.2 0.1 copy.38
  157.3 2.5 copy.37
  159.8 7.1 %pad_maximum_fusion = bf16[768,2,2048]{2,0,1:T(8,128)(2,1)} fusion(bf16[128,2,2048]{2,0,1:T(8,128)(2,1)S(1)} %bitcast.157, bf16[512,2,2048]{2,0,1:T(8,128)(2,1)S(1)} %bitcast.151, bf16[128,2,2048]{2,0,1:T(8,128)(2,1)S(1)} %bitcast.156), kind=kLoop, calls=%fused_computation.11 | loop fusion | flops 18874368 | bytes 12582912 | tf_op jit(solution)/shard_map/concatenate | solution.py:49
  166.9 23.6 %while.10 = (s32[]{:T(128)}, bf16[4,128,2,2048]{3,1,0,2:T(8,128)(2,1)}, s32[4]{0:T(128)S(1)}, bf16[768,2,2048]{2,0,1:T(8,128)(2,1)}, bf16[2,128,2,384]{3,1,2,0:T...) while((s32[]{:T(128)}, bf16[4,128,2,2048]{3,1,0,2:T(8,128)(2,1)}, s32[4]{0:T(128)S(1)}, ...), condition=%wide.region_1.2_spmd, body=%wide.region_0.1_spmd.sunk | while | flops 805830656 | bytes 8781991 | solution.py:57
  166.9 0.6 dynamic_slice.20
  168.3 2.9 fusion.72
  171.2 0.5 copy.66
  171.7 1.1 constant_dynamic-update-slice_fusion.2
  172.9 0.6 dynamic_slice.20
  174.2 2.9 fusion.72
  177.2 0.5 copy.66
  177.7 1.1 constant_dynamic-update-slice_fusion.2
  178.8 0.6 dynamic_slice.20
  180.2 2.9 fusion.72
  183.1 0.5 copy.66
  183.6 1.0 constant_dynamic-update-slice_fusion.2
  184.7 0.6 dynamic_slice.20
  186.0 2.9 fusion.72
  188.9 0.5 copy.66
  189.5 1.1 constant_dynamic-update-slice_fusion.2
  190.5 6.5 %copy.41 = bf16[512,2,2048]{2,1,0:T(2,128)(2,1)S(1)} copy(bf16[512,2,2048]{2,0,1:T(8,128)(2,1)} %bitcast.159) | data formatting | bytes 8388608 | tf_op jit(solution)/shard_map/reshape | solution.py:58
  197.0 99.6 %all_to_all.20 = bf16[512,2,2048]{2,1,0:T(2,128)(2,1)S(1)} all-to-all(bf16[512,2,2048]{2,1,0:T(2,128)(2,1)S(1)} %copy.41), channel_id=1, replica_groups=mesh['ma'=16,'ch'=2] {'ma'}, dimensions={0} | all-to-all | bytes 8388608 | tf_op jit(solution)/shard_map/all_to_all | solution.py:59
  296.7 5.4 %copy.64 = bf16[16,32,2,2048]{3,0,2,1:T(8,128)(2,1)} copy(bf16[16,32,2,2048]{3,2,1,0:T(2,128)(2,1)S(1)} %bitcast.153) | data formatting | bytes 8388608 | tf_op jit(solution)/shard_map/all_to_all | solution.py:59
  302.1 7.4 %reshape.93 = bf16[32,2,256,128]{3,2,1,0:T(8,128)(2,1)} reshape(bf16[32,2,16,2048]{3,2,1,0:T(8,128)(2,1)} %bitcast.154) | data formatting | bytes 8388608 | tf_op jit(solution)/shard_map/reshape | solution.py:60
  309.5 6.4 %copy.43 = bf16[32,2,256,128]{2,3,1,0:T(8,128)(2,1)} copy(bf16[32,2,256,128]{3,2,1,0:T(8,128)(2,1)} %reshape.93) | data formatting | bytes 8388608 | tf_op jit(solution)/shard_map/reshape | solution.py:60
  315.9 16.4 %all-gather.2.cloned.1.call-done = bf16[32,512,2,128]{1,3,2,0:T(8,128)(2,1)} async-done(((bf16[32,256,2,128]{1,3,2,0:T(8,128)(2,1)}), bf16[32,512,2,128]{1,3,2,0:T(8,128)(2,1)}) %all-gather.2.cloned.1.call-update) | async-done | bytes 8388624 | tf_op jit(solution)/shard_map/all_gather | solution.py:64
  332.4 11.4 %fusion.16 = f32[32,128,2,2,128]{1,4,2,3,0:T(8,128)} fusion(bf16[32,128,2,512,1]{3,2,1,0,4:T(2,128)(2,1)} %bitcast.155, bf16[32,512,2,128]{1,3,2,0:T(8,128)(2,1)} %all-gather.2.cloned.1.call-done), kind=kOutput, calls=%fused_computation.13 | convolution fusion | flops 2147483648 | bytes 25165824 | tf_op jit(solution)/shard_map/mkqc,mcrs->mkqrs/dot_general | solution.py:61
  343.7 2.6 fusion.25
  346.3 2.6 fusion.24
  348.9 0.2 pad_maximum_fusion.1
  349.1 3.8 %copy.47 = bf16[32,128,2,128]{3,2,1,0:T(2,128)(2,1)} copy(bf16[32,128,2,128]{1,3,0,2:T(8,128)(2,1)S(1)} %pad_maximum_fusion.1) | data formatting | bytes 4194304 | tf_op jit(solution)/shard_map/stack | solution.py:69
  (19 shorter events, 0.2 us)
Async XLA Ops:
  45.8 8.6 %copy-start.1 = (u32[32]{0:T(128)S(1)}, u32[32]{0:T(128)}, u32[]{:S(2)}) copy-start(u32[32]{0:T(128)} %constant.52) | copy-start | bytes 388
  45.8 9.8 %copy-start = (s32[32]{0:T(128)S(1)}, s32[32]{0:T(128)}, u32[]{:S(2)}) copy-start(s32[32]{0:T(128)} %param.7) | copy-start | bytes 388
  45.8 109.6 %all-to-all-start = ((bf16[16,32,2,2048]{3,1,2,0:T(8,128)(2,1)}), bf16[16,32,2,2048]{3,1,2,0:T(8,128)(2,1)}, u32[]{:S(2)}, u32[]{:S(2)}) async-start(bf16[16,32,2,2048]{3,1,2,0:T(8,128)(2,1)} %fusion.37), calls=%async_computation | async-start | bytes 8388608 | tf_op jit(solution)/shard_map/all_to_all | solution.py:44
  54.4 278.0 %all-gather.2.cloned.1.call-start = ((), (), s32[]{:S(2)}) async-start(), calls=%async_computation.2 | async-start | bytes 12582912 | tf_op jit(solution)/shard_map/all_gather | solution.py:64
Sparse Core Ops, SparseCore 0:
  316.0 16.2 all-gather.1
